TPU v7x, 128 devices: a whole 4x4x4 slice. The times are simulated.
128 devices in a mesh: seq: 32 (over y, z, core), chan: 4 (over x).
Axes of the slice: x: 4, y: 4, z: 4, core: 2. Of those that a mesh axis runs over, the one named last changes fastest.
Arguments:
- tokens: bfloat16 [16384, 4096], P('seq', 'chan'), may hold values from -6 to 6
- in_weight: bfloat16 [4096, 3, 2048], P(None, None, 'chan'), may hold values from -0.09375 to 0.09375
- short_weight: float32 [3, 3, 2048], P(None, None, 'chan'), may hold values from -3 to 3
- filter_taps: float32 [16384, 2048], P('seq', 'chan'), may hold values from -1.1 to 1.1
- skip_gain: float32 [2048], P('chan'), may hold values from -3 to 3
Outputs:
- hyena_out: bfloat16 [16384, 2048], P('seq', 'chan')
All inputs are finite; a program needn't handle non-finite values.
Results may differ from a plain program's by a relative error of at most 0.012.
Values may be sent and summed in bfloat16 or wider, within the bound.
A program may use at most 128 MiB of HBM per device.

v0:
```python
import jax
import jax.numpy as jnp
import numpy as np
from jax import lax
from jax.sharding import PartitionSpec as P

exact = lax.Precision.HIGHEST
SIDE = 128


def transform_tables():
    n = np.arange(SIDE)
    odd = n + 0.5
    first = -2.0 * np.pi / (2 * SIDE) * np.outer(odd, n)
    turn = -2.0 * np.pi / (2 * SIDE * SIDE) * np.outer(odd, n)
    second = -2.0 * np.pi / SIDE * np.outer(n, n)
    wide = np.concatenate([np.cos(first), np.sin(first)], 0)
    cos2, sin2 = (np.cos(second), np.sin(second))
    mix = np.block([[cos2, sin2], [-sin2, cos2]])
    back = np.block([[cos2, -sin2], [sin2, cos2]]) / (SIDE * SIDE)
    return [np.asarray(a, np.float32) for a in (wide, np.cos(turn), np.sin(turn), mix, back)]


def forward(x, tables):
    wide, cosine, sine, mix, _ = tables
    a = jnp.einsum("kn,cnm->ckm", wide, x, precision=exact)
    re, im = (a[:, :SIDE], a[:, SIDE:])
    turned = jnp.concatenate([re * cosine - im * sine, re * sine + im * cosine], axis=2)
    b = jnp.einsum("ckm,mf->ckf", turned, mix, precision=exact)
    return (b[:, :, :SIDE], b[:, :, SIDE:])


def inverse(re, im, tables):
    wide, cosine, sine, _, back = tables
    c = jnp.einsum("ckf,fm->ckm", jnp.concatenate([re, im], axis=2), back, precision=exact)
    re, im = (c[:, :, :SIDE], c[:, :, SIDE:])
    turned = jnp.concatenate([re * cosine + im * sine, im * cosine - re * sine], axis=1)
    return jnp.einsum("kn,ckm->cnm", wide, turned, precision=exact)


def local(tokens, in_weight, short_weight, filter_taps, skip_gain):
    rows, channels = filter_taps.shape
    seq_count = lax.axis_size("seq")
    own = channels // seq_count
    tables = transform_tables()

    def to_channels(values):
        parts = values.astype(jnp.bfloat16).T.reshape(seq_count, own, rows)
        parts = lax.all_to_all(parts, "seq", 0, 0, tiled=True)
        return parts.astype(jnp.float32).transpose(1, 0, 2).reshape(own, SIDE, SIDE)

    filter_re, filter_im = forward(to_channels(filter_taps), tables)
    projected = jnp.einsum(
        "td,dgc->tgc",
        lax.all_gather(tokens, "chan", axis=1, tiled=True),
        in_weight,
        preferred_element_type=jnp.float32,
    ).astype(jnp.bfloat16)
    pairs = [(i, i + 1) for i in range(seq_count - 1)]
    previous = lax.ppermute(projected[rows - 2 :], "seq", pairs)
    extended = jnp.concatenate([previous, projected], axis=0).astype(jnp.float32)
    shorted = (
        short_weight[0] * extended[2:]
        + short_weight[1] * extended[1:-1]
        + short_weight[2] * extended[:-2]
    ).astype(jnp.bfloat16)
    short_f32 = shorted.astype(jnp.float32)
    mixed_in = short_f32[:, 1] * short_f32[:, 2]
    data_re, data_im = forward(to_channels(mixed_in), tables)
    prod_re = data_re * filter_re - data_im * filter_im
    prod_im = data_re * filter_im + data_im * filter_re
    result = inverse(prod_re, prod_im, tables)
    parts = result.reshape(own, seq_count, rows).transpose(1, 0, 2).astype(jnp.bfloat16)
    parts = lax.all_to_all(parts, "seq", 0, 0, tiled=True)
    conv_vals = parts.reshape(channels, rows).T.astype(jnp.float32)
    return ((conv_vals + skip_gain * mixed_in) * short_f32[:, 0]).astype(jnp.bfloat16)


def solution(mesh):
    return jax.shard_map(
        local,
        mesh=mesh,
        in_specs=(
            P("seq", "chan"),
            P(None, None, "chan"),
            P(None, None, "chan"),
            P("seq", "chan"),
            P("chan"),
        ),
        out_specs=P("seq", "chan"),
        check_vma=False,
    )
```

profile of v0, /device:TPU:1, one launch (start us, length us, event | category | flops | bytes accessed | tf_op | source)
XLA Modules:
  0.0 156.6 jit_solution(4305946872558617440)
XLA Ops:
  7.3 2.2 %copy.35 = bf16[512,512]{0,1:T(8,128)(2,1)} copy(f32[512,512]{1,0:T(8,128)} %param.16) | data formatting | bytes 1572864 | tf_op args[3]
  9.5 9.6 %all-to-all-start.1 = ((bf16[32,16,512]{2,1,0:T(8,128)(2,1)}), bf16[32,16,512]{2,1,0:T(8,128)(2,1)}, u32[]{:S(2)}, u32[]{:S(2)}) async-start(bf16[32,16,512]{2,1,0:T(8,128)(2,1)} %bitcast.12), calls=%async_computation.1 | async-start | bytes 1048576 | tf_op jit(solution)/shard_map/all_to_all | solution.py:49
  19.2 41.1 %all-gather.2.cloned.1.call-done = bf16[512,4096]{1,0:T(8,128)(2,1)} async-done(((bf16[512,1024]{1,0:T(8,128)(2,1)}), bf16[512,4096]{1,0:T(8,128)(2,1)}) %all-gather.2.cloned.1.call-update) | async-done | bytes 4194320 | tf_op jit(solution)/shard_map/all_gather | solution.py:55
  60.2 10.9 %fusion.21 = bf16[512,3,512]{2,0,1:T(8,128)(2,1)S(1)} fusion(bf16[4096,3,512]{2,0,1:T(8,128)(2,1)} %param.14, bf16[512,4096]{1,0:T(8,128)(2,1)} %all-gather.2.cloned.1.call-done), kind=kOutput, calls=%fused_computation.24 | convolution fusion | flops 6443237376 | bytes 18350080 | tf_op jit(solution)/shard_map/td,dgc->tgc/dot_general | solution.py:53
  71.1 3.9 %collective-permute-start = (bf16[2,3,512]{2,0,1:T(2,128)(2,1)S(1)}, bf16[2,3,512]{2,0,1:T(2,128)(2,1)S(1)}, u32[]{:S(2)}, u32[]{:S(2)}) collective-permute-start(bf16[2,3,512]{2,0,1:T(2,128)(2,1)S(1)} %slice.80), channel_id=1, source_target_pairs={{0,4},{4,8},{8,12},{12,16},{16,20},{20,24},{24,28},{28,32},{32,36}... | collective-permute-start | bytes 18440 | tf_op jit(solution)/shard_map/ppermute | solution.py:60
  78.2 2.0 %copy.31 = bf16[512,512]{1,0:T(8,128)(2,1)} copy(bf16[512,512]{0,1:T(8,128)(2,1)} %convert_bitcast_fusion) | data formatting | bytes 1048576 | tf_op jit(solution)/shard_map/transpose | solution.py:48
  80.2 8.5 %all-to-all-start = ((bf16[32,16,512]{2,1,0:T(8,128)(2,1)}), bf16[32,16,512]{2,1,0:T(8,128)(2,1)}, u32[]{:S(2)}, u32[]{:S(2)}) async-start(bf16[32,16,512]{2,1,0:T(8,128)(2,1)} %bitcast.62), calls=%async_computation | async-start | bytes 1048576 | tf_op jit(solution)/shard_map/all_to_all | solution.py:49
  88.8 2.1 %copy.36 = bf16[16,32,512]{2,1,0:T(8,128)(2,1)} copy(bf16[16,32,512]{2,0,1:T(8,128)(2,1)} %bitcast.13) | data formatting | bytes 1048576 | tf_op jit(solution)/shard_map/transpose | solution.py:50
  90.9 2.1 %reshape.24 = bf16[16,128,128]{2,1,0:T(8,128)(2,1)} reshape(bf16[16,32,512]{2,1,0:T(8,128)(2,1)} %copy.36) | data formatting | bytes 1048576 | tf_op jit(solution)/shard_map/reshape | solution.py:50
  93.0 2.0 %copy.37 = bf16[16,128,128]{1,2,0:T(8,128)(2,1)} copy(bf16[16,128,128]{2,1,0:T(8,128)(2,1)} %reshape.24) | data formatting | bytes 1048576 | tf_op jit(solution)/shard_map/reshape | solution.py:50
  95.1 3.4 %fusion.38 = f32[256,2048]{0,1} fusion(f32[256,128]{1,0:T(8,128)S(1)} %copy-done.6, bf16[128,2048]{0,1:T(8,128)(2,1)} %bitcast.64), kind=kOutput, calls=%fused_computation.53 | convolution fusion | flops 805306368 | bytes 2752512
  98.5 1.7 %all-to-all-done = bf16[32,16,512]{2,1,0:T(8,128)(2,1)} async-done(((bf16[32,16,512]{2,1,0:T(8,128)(2,1)}), bf16[32,16,512]{2,1,0:T(8,128)(2,1)}, u32[]{:S(2)}, u32[]{:S(2)}) %all-to-all-start) | async-done | bytes 524320 | tf_op jit(solution)/shard_map/all_to_all | solution.py:49
  100.2 2.1 %copy.32 = bf16[16,32,512]{2,1,0:T(8,128)(2,1)} copy(bf16[16,32,512]{2,0,1:T(8,128)(2,1)} %bitcast.7) | data formatting | bytes 1048576 | tf_op jit(solution)/shard_map/transpose | solution.py:50
  102.3 2.2 %reshape.22 = bf16[16,128,128]{2,1,0:T(8,128)(2,1)} reshape(bf16[16,32,512]{2,1,0:T(8,128)(2,1)} %copy.32) | data formatting | bytes 1048576 | tf_op jit(solution)/shard_map/reshape | solution.py:50
  104.5 2.2 %convolution_bitcast_fusion = f32[16,256,128]{1,2,0:T(8,128)S(1)} fusion(bf16[16,128,128]{2,1,0:T(8,128)(2,1)} %reshape.22, f32[256,128,1]{1,0,2:T(8,128)S(1)} %copy-done.2), kind=kOutput, calls=%fused_computation.25 | convolution fusion | flops 805306368 | bytes 2752512 | tf_op jit(solution)/shard_map/kn,cnm->ckm/dot_general | solution.py:26
  107.8 3.5 %fusion.5 = f32[16,128,256]{2,1,0:T(8,128)S(1)} fusion(f32[256,256,1]{1,0,2:T(8,128)S(1)} %copy-done.1, f32[16,128,128]{1,2,0:T(8,128)S(1)} %get-tuple-element.10, f32[16,128,128]{1,2,0:T(8,128)S(1)} %get-tuple-element.9), kind=kOutput, calls=%fused_computation.8 | convolution fusion | flops 1611137024 | bytes 4456448 | tf_op jit(solution)/shard_map/ckm,mf->ckf/dot_general | solution.py:29
  111.3 3.4 %fusion.9 = f32[16,128,256]{2,1,0:T(8,128)S(1)} fusion(f32[256,256,1]{1,0,2:T(8,128)S(1)} %copy-done.1, f32[16,128,128]{1,2,0:T(8,128)S(1)} %get-tuple-element.13, f32[16,128,128]{1,2,0:T(8,128)S(1)} %get-tuple-element.14), kind=kOutput, calls=%fused_computation.12 | convolution fusion | flops 1611137024 | bytes 4456448 | tf_op jit(solution)/shard_map/ckm,mf->ckf/dot_general | solution.py:29
  115.7 2.3 %fusion.13 = f32[16,128,256]{1,2,0:T(8,128)S(1)} fusion(f32[256,256,1]{1,0,2:T(8,128)S(1)} %copy-done.5, f32[16,128,128]{2,1,0:T(8,128)S(1)} %get-tuple-element.6, f32[16,128,128]{2,1,0:T(8,128)S(1)} %get-tuple-element.5), kind=kOutput, calls=%fused_computation.16 | convolution fusion | flops 1611137024 | bytes 4456448 | tf_op jit(solution)/shard_map/ckf,fm->ckm/dot_general | solution.py:35
  118.4 2.6 %fusion.28 = bf16[16,128,128]{1,2,0:T(8,128)(2,1)} fusion(f32[256,128,1]{1,0,2:T(8,128)S(1)} %copy-done.2, f32[16,128,128]{1,2,0:T(8,128)S(1)} %get-tuple-element.8, f32[16,128,128]{1,2,0:T(8,128)S(1)} %get-tuple-element.7), kind=kOutput, calls=%fused_computation.29 | convolution fusion | flops 806092800 | bytes 2752512 | tf_op jit(solution)/shard_map/kn,ckm->cnm/dot_general | solution.py:38
  121.0 2.0 %copy.41 = bf16[16,128,128]{2,1,0:T(8,128)(2,1)} copy(bf16[16,128,128]{1,2,0:T(8,128)(2,1)} %fusion.28) | data formatting | bytes 1048576 | tf_op jit(solution)/shard_map/convert_element_type | solution.py:73
  123.0 2.1 %convert_element_type.52 = bf16[16,32,512]{2,1,0:T(8,128)(2,1)} reshape(bf16[16,128,128]{2,1,0:T(8,128)(2,1)} %copy.41) | data formatting | bytes 1048576 | tf_op jit(solution)/shard_map/convert_element_type | solution.py:73
  126.5 17.0 %all_to_all.15 = bf16[32,16,512]{2,1,0:T(8,128)(2,1)S(1)} all-to-all(bf16[32,16,512]{2,1,0:T(8,128)(2,1)S(1)} %copy.42), channel_id=1, replica_groups=mesh['seq'=32,'chan'=4] {'seq'}, dimensions={0} | all-to-all | bytes 1048576 | tf_op jit(solution)/shard_map/all_to_all | solution.py:74
  144.7 2.5 %copy.43 = f32[512,512]{0,1:T(8,128)} copy(f32[512,512]{1,0:T(8,128)} %bitcast_convert_fusion) | data formatting | bytes 2097152 | tf_op jit(solution)/shard_map/convert_element_type | solution.py:75
  147.2 2.5 %fusion.32 = bf16[512,512]{1,0:T(8,128)(2,1)} fusion(f32[512,3,512]{2,0,1:T(8,128)S(1)} %fusion.24, f32[512,512]{0,1:T(8,128)} %copy.43, f32[512]{0:T(512)S(1)} %copy-done.8), kind=kLoop, calls=%fused_computation.32 | loop fusion | flops 1310720 | bytes 4720640 | tf_op jit(solution)/shard_map/convert_element_type | solution.py:76
  (32 shorter events, 8.5 us)
Async XLA Ops:
  6.5 53.7 %all-gather.2.cloned.1.call-start = ((), (), s32[]{:S(2)}) async-start(), calls=%async_computation.3 | async-start | bytes 5242880 | tf_op jit(solution)/shard_map/all_gather | solution.py:55
  9.5 70.7 %all-to-all-start.1 = ((bf16[32,16,512]{2,1,0:T(8,128)(2,1)}), bf16[32,16,512]{2,1,0:T(8,128)(2,1)}, u32[]{:S(2)}, u32[]{:S(2)}) async-start(bf16[32,16,512]{2,1,0:T(8,128)(2,1)} %bitcast.12), calls=%async_computation.1 | async-start | bytes 1048576 | tf_op jit(solution)/shard_map/all_to_all | solution.py:49
  19.1 55.9 %copy-start.7 = (f32[3,3,512]{2,1,0:T(4,128)S(1)}, f32[3,3,512]{2,1,0:T(4,128)}, u32[]{:S(2)}) copy-start(f32[3,3,512]{2,1,0:T(4,128)} %param.15) | copy-start | bytes 55300
  71.1 4.7 %collective-permute-start = (bf16[2,3,512]{2,0,1:T(2,128)(2,1)S(1)}, bf16[2,3,512]{2,0,1:T(2,128)(2,1)S(1)}, u32[]{:S(2)}, u32[]{:S(2)}) collective-permute-start(bf16[2,3,512]{2,0,1:T(2,128)(2,1)S(1)} %slice.80), channel_id=1, source_target_pairs={{0,4},{4,8},{8,12},{12,16},{16,20},{20,24},{24,28},{28,32},{32,36}... | collective-permute-start | bytes 18440 | tf_op jit(solution)/shard_map/ppermute | solution.py:60
  80.2 14.9 %copy-start.6 = (f32[256,128]{1,0:T(8,128)S(1)}, f32[256,128]{1,0:T(8,128)}, u32[]{:S(2)}) copy-start(f32[256,128]{1,0:T(8,128)} %constant.10.clone) | copy-start | bytes 393220
  80.2 20.0 %all-to-all-start = ((bf16[32,16,512]{2,1,0:T(8,128)(2,1)}), bf16[32,16,512]{2,1,0:T(8,128)(2,1)}, u32[]{:S(2)}, u32[]{:S(2)}) async-start(bf16[32,16,512]{2,1,0:T(8,128)(2,1)} %bitcast.62), calls=%async_computation | async-start | bytes 1048576 | tf_op jit(solution)/shard_map/all_to_all | solution.py:49
  95.1 9.5 %copy-start.2 = (f32[256,128,1]{1,0,2:T(8,128)S(1)}, f32[256,128,1]{1,0,2:T(8,128)}, u32[]{:S(2)}) copy-start(f32[256,128,1]{1,0,2:T(8,128)} %constant.15) | copy-start | bytes 393220
  102.3 4.4 %copy-start.3 = (f32[128,128]{0,1:T(8,128)S(1)}, f32[128,128]{0,1:T(8,128)}, u32[]{:S(2)}) copy-start(f32[128,128]{0,1:T(8,128)} %constant.12.clone) | copy-start | bytes 196612
  102.3 4.4 %copy-start.4 = (f32[128,128]{0,1:T(8,128)S(1)}, f32[128,128]{0,1:T(8,128)}, u32[]{:S(2)}) copy-start(f32[128,128]{0,1:T(8,128)} %constant.11.clone) | copy-start | bytes 196612
  104.5 2.3 %copy-start = (f32[256,2048]{0,1:S(1)}, f32[256,2048]{0,1}, u32[]{:S(2)}) copy-start(f32[256,2048]{0,1} %fusion.38) | copy-start | bytes 6291460
  106.8 1.0 copy-start.1
  114.8 1.0 copy-start.5
  143.5 3.7 %copy-start.8 = (f32[512]{0:T(512)S(1)}, f32[512]{0:T(512)}, u32[]{:S(2)}) copy-start(f32[512]{0:T(512)} %param.17) | copy-start | bytes 6148
Sparse Core Ops, SparseCore 0:
  9.0 51.1 all-gather.1
where the time goes:
time: 158 us; the launch traced here: 157 us
  waiting for transfers between devices  44.3 us (28%)
  matrix products  28.4 us (18%)
  local copies, waits for them, and re-layouts  23.9 us (15%)
  starting transfers between devices  22.1 us (14%)
  blocking collectives  17 us (11%)
  between operations  13.6 us (9%)
  other arithmetic  7.3 us (5%)
    all_gather x1, waiting for transfers between devices, local(): lax.all_gather(tokens, 'chan', axis=1, tiled=True)  41.1 us
    all_to_all x2, starting transfers between devices, to_channels(): parts = lax.all_to_all(parts, 'seq', 0, 0, tiled=True)  18.2 us
    all_to_all x1, blocking collectives, local(): parts = lax.all_to_all(parts, 'seq', 0, 0, tiled=True)  17 us
    dot_general x1, matrix products, local(): jnp.einsum('td,dgc->tgc', lax.all_gather(tokens, 'chan', axis=1, tiled=Tr...  10.9 us
    dot_general x2, matrix products, forward(): b = jnp.einsum('ckm,mf->ckf', turned, mix, precision=exact)  6.98 us
    reshape x3, local copies, waits for them, and re-layouts, to_channels(): return parts.astype(jnp.float32).transpose(1, 0, 2).reshape(own, SIDE, SIDE)  6.37 us
    convert_element_type x3, local copies, waits for them, and re-layouts, local(): result.reshape(own, seq_count, rows).transpose(1, 0, 2).astype(jnp.bfloat16)  5.52 us
    transpose x2, local copies, waits for them, and re-layouts, to_channels(): return parts.astype(jnp.float32).transpose(1, 0, 2).reshape(own, SIDE, SIDE)  4.25 us
  transfers between devices with their start and end apart: 4, of which 3 were waited for; matrix products, arithmetic and copies ran while one was open for 17% of the time, Pallas kernels for 0%

commit v1 on v0

--- a/solution.py
+++ b/solution.py
@@ -6,6 +6,11 @@
 
 exact = lax.Precision.HIGHEST
 SIDE = 128
+
+
+def swapped_in(x, name, dim):
+    repeated = jnp.stack([x] * lax.axis_size(name))
+    return jnp.concatenate(lax.all_to_all(repeated, name, 0, 0), axis=dim)
 
 
 def transform_tables():
@@ -51,10 +56,7 @@
 
     filter_re, filter_im = forward(to_channels(filter_taps), tables)
     projected = jnp.einsum(
-        "td,dgc->tgc",
-        lax.all_gather(tokens, "chan", axis=1, tiled=True),
-        in_weight,
-        preferred_element_type=jnp.float32,
+        "td,dgc->tgc", swapped_in(tokens, "chan", 1), in_weight, preferred_element_type=jnp.float32
     ).astype(jnp.bfloat16)
     pairs = [(i, i + 1) for i in range(seq_count - 1)]
     previous = lax.ppermute(projected[rows - 2 :], "seq", pairs)

time: 158 us -> 173 us (1.095)
  local copies, waits for them, and re-layouts: 23.9 us -> 41.7 us
  between operations: 13.6 us -> 0.2 us
  waiting for transfers between devices: 44.3 us -> 50.2 us
  starting transfers between devices: 22.1 us -> 27 us
    all_to_all x0 -> x1, waiting for transfers between devices: none -> 47.7 us  [swapped_in(): return jnp.concatenate(lax.all_to_all(repeated, name, 0, 0), axis=dim)]
    all_gather x1 -> x0, waiting for transfers between devices: 41.1 us -> none  [local(): lax.all_gather(tokens, 'chan', axis=1, tiled=True)]
    reshape x0 -> x2, local copies, waits for them, and re-layouts: none -> 15.1 us  [swapped_in(): return jnp.concatenate(lax.all_to_all(repeated, name, 0, 0), axis=dim)]
    all_to_all x0 -> x1, starting transfers between devices: none -> 4.99 us  [swapped_in(): return jnp.concatenate(lax.all_to_all(repeated, name, 0, 0), axis=dim)]
    another operation x0 -> x1, local copies, waits for them, and re-layouts: none -> 3.75 us  [swapped_in(): repeated = jnp.stack([x] * lax.axis_size(name))]
  transfers between devices with their start and end apart: 4 -> 4, of which waited for: 3 -> 3; matrix products, arithmetic and copies ran while one was open for 17% -> 24% of each run, Pallas kernels for 0% -> 0%
where the time goes in v1:
time: 173 us; the launch traced here: 172 us
  waiting for transfers between devices  50.2 us (29%)
  local copies, waits for them, and re-layouts  41.7 us (24%)
  matrix products  28.5 us (16%)
  starting transfers between devices  27 us (16%)
  blocking collectives  17 us (10%)
  other arithmetic  7.28 us (4%)
    all_to_all x1, waiting for transfers between devices, swapped_in(): return jnp.concatenate(lax.all_to_all(repeated, name, 0, 0), axis=dim)  47.7 us
    all_to_all x2, starting transfers between devices, to_channels(): parts = lax.all_to_all(parts, 'seq', 0, 0, tiled=True)  18.4 us
    all_to_all x1, blocking collectives, local(): parts = lax.all_to_all(parts, 'seq', 0, 0, tiled=True)  17 us
    reshape x2, local copies, waits for them, and re-layouts, swapped_in(): return jnp.concatenate(lax.all_to_all(repeated, name, 0, 0), axis=dim)  15.1 us
    dot_general x1, matrix products, local(): jnp.einsum('td,dgc->tgc', swapped_in(tokens, 'chan', 1), in_weight, prefe...  10.9 us
    dot_general x2, matrix products, forward(): b = jnp.einsum('ckm,mf->ckf', turned, mix, precision=exact)  7.08 us
    reshape x3, local copies, waits for them, and re-layouts, to_channels(): return parts.astype(jnp.float32).transpose(1, 0, 2).reshape(own, SIDE, SIDE)  6.37 us
    convert_element_type x3, local copies, waits for them, and re-layouts, local(): result.reshape(own, seq_count, rows).transpose(1, 0, 2).astype(jnp.bfloat16)  5.52 us
  transfers between devices with their start and end apart: 4, of which 3 were waited for; matrix products, arithmetic and copies ran while one was open for 24% of the time, Pallas kernels for 0%

profile of v1, /device:TPU:1, one launch (start us, length us, event | category | flops | bytes accessed | tf_op | source)
XLA Modules:
  0.0 171.8 jit_solution(3375410867099144503)
XLA Ops:
  0.0 3.7 %stack.2 = bf16[4,512,1024]{2,1,0:T(8,128)(2,1)} broadcast(bf16[512,1024]{1,0:T(8,128)(2,1)} %param.13), dimensions={1,2} | broadcast | bytes 5242880 | tf_op jit(solution)/shard_map/stack | solution.py:12
  3.8 5.0 %all-to-all-start = ((bf16[4,512,1024]{2,1,0:T(8,128)(2,1)}), bf16[4,512,1024]{2,1,0:T(8,128)(2,1)}, u32[]{:S(2)}, u32[]{:S(2)}) async-start(bf16[4,512,1024]{2,1,0:T(8,128)(2,1)} %stack.2), calls=%async_computation | async-start | bytes 8388608 | tf_op jit(solution)/shard_map/all_to_all | solution.py:13
  9.8 47.7 %all-to-all-done = bf16[4,512,1024]{2,1,0:T(8,128)(2,1)} async-done(((bf16[4,512,1024]{2,1,0:T(8,128)(2,1)}), bf16[4,512,1024]{2,1,0:T(8,128)(2,1)}, u32[]{:S(2)}, u32[]{:S(2)}) %all-to-all-start) | async-done | bytes 4194336 | tf_op jit(solution)/shard_map/all_to_all | solution.py:13
  57.5 10.0 %all-to-all-start.2 = ((bf16[32,16,512]{2,1,0:T(8,128)(2,1)}), bf16[32,16,512]{2,1,0:T(8,128)(2,1)}, u32[]{:S(2)}, u32[]{:S(2)}) async-start(bf16[32,16,512]{2,1,0:T(8,128)(2,1)} %bitcast.12), calls=%async_computation.2 | async-start | bytes 1048576 | tf_op jit(solution)/shard_map/all_to_all | solution.py:54
  67.5 7.4 %copy.31 = bf16[512,4,1024]{2,1,0:T(4,128)(2,1)} copy(bf16[512,4,1024]{2,0,1:T(8,128)(2,1)} %bitcast.1) | data formatting | bytes 8388608 | tf_op jit(solution)/shard_map/reshape | solution.py:13
  74.9 7.7 %reshape.36 = bf16[512,4096,1]{1,0,2:T(8,128)(2,1)} reshape(bf16[512,4,1024]{2,1,0:T(4,128)(2,1)} %copy.31) | data formatting | bytes 8388608 | tf_op jit(solution)/shard_map/reshape | solution.py:13
  82.7 10.9 %convolution_convert_fusion = bf16[512,3,512]{2,0,1:T(8,128)(2,1)S(1)} fusion(bf16[512,4096,1]{1,0,2:T(8,128)(2,1)} %reshape.36, bf16[4096,3,512]{2,0,1:T(8,128)(2,1)} %param.14), kind=kOutput, calls=%fused_computation.22 | convolution fusion | flops 6443237376 | bytes 18350080 | tf_op jit(solution)/shard_map/td,dgc->tgc/dot_general | solution.py:58
  93.6 3.5 %collective-permute-start = (bf16[2,3,512]{2,0,1:T(2,128)(2,1)S(1)}, bf16[2,3,512]{2,0,1:T(2,128)(2,1)S(1)}, u32[]{:S(2)}, u32[]{:S(2)}) collective-permute-start(bf16[2,3,512]{2,0,1:T(2,128)(2,1)S(1)} %slice.80), channel_id=1, source_target_pairs={{0,4},{4,8},{8,12},{12,16},{16,20},{20,24},{24,28},{28,32},{32,36}... | collective-permute-start | bytes 18440 | tf_op jit(solution)/shard_map/ppermute | solution.py:62
  100.3 2.0 %copy.32 = bf16[512,512]{1,0:T(8,128)(2,1)} copy(bf16[512,512]{0,1:T(8,128)(2,1)} %convert_bitcast_fusion) | data formatting | bytes 1048576 | tf_op jit(solution)/shard_map/transpose | solution.py:53
  102.3 8.4 %all-to-all-start.1 = ((bf16[32,16,512]{2,1,0:T(8,128)(2,1)}), bf16[32,16,512]{2,1,0:T(8,128)(2,1)}, u32[]{:S(2)}, u32[]{:S(2)}) async-start(bf16[32,16,512]{2,1,0:T(8,128)(2,1)} %bitcast.59), calls=%async_computation.1 | async-start | bytes 1048576 | tf_op jit(solution)/shard_map/all_to_all | solution.py:54
  110.7 2.1 %copy.37 = bf16[16,32,512]{2,1,0:T(8,128)(2,1)} copy(bf16[16,32,512]{2,0,1:T(8,128)(2,1)} %bitcast.13) | data formatting | bytes 1048576 | tf_op jit(solution)/shard_map/transpose | solution.py:55
  112.9 2.1 %reshape.34 = bf16[16,128,128]{2,1,0:T(8,128)(2,1)} reshape(bf16[16,32,512]{2,1,0:T(8,128)(2,1)} %copy.37) | data formatting | bytes 1048576 | tf_op jit(solution)/shard_map/reshape | solution.py:55
  117.1 3.4 %fusion.33 = f32[256,2048]{0,1} fusion(f32[256,128]{1,0:T(8,128)S(1)} %copy-done.7, bf16[128,2048]{0,1:T(8,128)(2,1)} %bitcast.61), kind=kOutput, calls=%fused_computation.51 | convolution fusion | flops 805306368 | bytes 2752512
  122.2 2.1 %copy.33 = bf16[16,32,512]{2,1,0:T(8,128)(2,1)} copy(bf16[16,32,512]{2,0,1:T(8,128)(2,1)} %bitcast.7) | data formatting | bytes 1048576 | tf_op jit(solution)/shard_map/transpose | solution.py:55
  124.3 2.2 %reshape.32 = bf16[16,128,128]{2,1,0:T(8,128)(2,1)} reshape(bf16[16,32,512]{2,1,0:T(8,128)(2,1)} %copy.33) | data formatting | bytes 1048576 | tf_op jit(solution)/shard_map/reshape | solution.py:55
  126.5 2.2 %convolution_bitcast_fusion = f32[16,256,128]{1,2,0:T(8,128)S(1)} fusion(bf16[16,128,128]{2,1,0:T(8,128)(2,1)} %reshape.32, f32[256,128,1]{1,0,2:T(8,128)S(1)} %copy-done.3), kind=kOutput, calls=%fused_computation.23 | convolution fusion | flops 805306368 | bytes 2752512 | tf_op jit(solution)/shard_map/kn,cnm->ckm/dot_general | solution.py:31
  129.7 3.5 %fusion.3 = f32[16,128,256]{2,1,0:T(8,128)S(1)} fusion(f32[256,256,1]{1,0,2:T(8,128)S(1)} %copy-done.1, f32[16,128,128]{1,2,0:T(8,128)S(1)} %get-tuple-element.10, f32[16,128,128]{1,2,0:T(8,128)S(1)} %get-tuple-element.9), kind=kOutput, calls=%fused_computation.6 | convolution fusion | flops 1611137024 | bytes 4456448 | tf_op jit(solution)/shard_map/ckm,mf->ckf/dot_general | solution.py:34
  133.3 3.5 %fusion.7 = f32[16,128,256]{2,1,0:T(8,128)S(1)} fusion(f32[256,256,1]{1,0,2:T(8,128)S(1)} %copy-done.1, f32[16,128,128]{1,2,0:T(8,128)S(1)} %get-tuple-element.13, f32[16,128,128]{1,2,0:T(8,128)S(1)} %get-tuple-element.14), kind=kOutput, calls=%fused_computation.10 | convolution fusion | flops 1611137024 | bytes 4456448 | tf_op jit(solution)/shard_map/ckm,mf->ckf/dot_general | solution.py:34
  137.8 2.3 %fusion.11 = f32[16,128,256]{1,2,0:T(8,128)S(1)} fusion(f32[256,256,1]{1,0,2:T(8,128)S(1)} %copy-done.6, f32[16,128,128]{2,1,0:T(8,128)S(1)} %get-tuple-element.6, f32[16,128,128]{2,1,0:T(8,128)S(1)} %get-tuple-element.5), kind=kOutput, calls=%fused_computation.14 | convolution fusion | flops 1611137024 | bytes 4456448 | tf_op jit(solution)/shard_map/ckf,fm->ckm/dot_general | solution.py:40
  140.4 2.6 %fusion.23 = bf16[16,128,128]{1,2,0:T(8,128)(2,1)} fusion(f32[256,128,1]{1,0,2:T(8,128)S(1)} %copy-done.3, f32[16,128,128]{1,2,0:T(8,128)S(1)} %get-tuple-element.8, f32[16,128,128]{1,2,0:T(8,128)S(1)} %get-tuple-element.7), kind=kOutput, calls=%fused_computation.27 | convolution fusion | flops 806092800 | bytes 2752512 | tf_op jit(solution)/shard_map/kn,ckm->cnm/dot_general | solution.py:43
  145.1 2.1 %convert_element_type.52 = bf16[16,32,512]{2,1,0:T(8,128)(2,1)} reshape(bf16[16,128,128]{2,1,0:T(8,128)(2,1)} %copy.42) | data formatting | bytes 1048576 | tf_op jit(solution)/shard_map/convert_element_type | solution.py:75
  148.6 17.0 %all_to_all.20 = bf16[32,16,512]{2,1,0:T(8,128)(2,1)S(1)} all-to-all(bf16[32,16,512]{2,1,0:T(8,128)(2,1)S(1)} %copy.43), channel_id=1, replica_groups=mesh['seq'=32,'chan'=4] {'seq'}, dimensions={0} | all-to-all | bytes 1048576 | tf_op jit(solution)/shard_map/all_to_all | solution.py:76
  166.8 2.5 %copy.44 = f32[512,512]{0,1:T(8,128)} copy(f32[512,512]{1,0:T(8,128)} %bitcast_convert_fusion) | data formatting | bytes 2097152 | tf_op jit(solution)/shard_map/convert_element_type | solution.py:77
  169.3 2.5 %fusion.27 = bf16[512,512]{1,0:T(8,128)(2,1)} fusion(f32[512,3,512]{2,0,1:T(8,128)S(1)} %fusion.19, f32[512,512]{0,1:T(8,128)} %copy.44, f32[512]{0:T(512)S(1)} %copy-done.9), kind=kLoop, calls=%fused_computation.30 | loop fusion | flops 1310720 | bytes 4720640 | tf_op jit(solution)/shard_map/convert_element_type | solution.py:78
  (36 shorter events, 14.7 us)
Async XLA Ops:
  3.8 5.0 %copy-start.2 = (f32[512,512]{1,0:T(8,128)S(1)}, f32[512,512]{1,0:T(8,128)}, u32[]{:S(2)}) copy-start(f32[512,512]{1,0:T(8,128)} %param.16) | copy-start | bytes 3145732
  3.8 53.8 %all-to-all-start = ((bf16[4,512,1024]{2,1,0:T(8,128)(2,1)}), bf16[4,512,1024]{2,1,0:T(8,128)(2,1)}, u32[]{:S(2)}, u32[]{:S(2)}) async-start(bf16[4,512,1024]{2,1,0:T(8,128)(2,1)} %stack.2), calls=%async_computation | async-start | bytes 8388608 | tf_op jit(solution)/shard_map/all_to_all | solution.py:13
  57.5 44.8 %all-to-all-start.2 = ((bf16[32,16,512]{2,1,0:T(8,128)(2,1)}), bf16[32,16,512]{2,1,0:T(8,128)(2,1)}, u32[]{:S(2)}, u32[]{:S(2)}) async-start(bf16[32,16,512]{2,1,0:T(8,128)(2,1)} %bitcast.12), calls=%async_computation.2 | async-start | bytes 1048576 | tf_op jit(solution)/shard_map/all_to_all | solution.py:54
  82.7 14.5 %copy-start.8 = (f32[3,3,512]{2,1,0:T(4,128)S(1)}, f32[3,3,512]{2,1,0:T(4,128)}, u32[]{:S(2)}) copy-start(f32[3,3,512]{2,1,0:T(4,128)} %param.15) | copy-start | bytes 55300
  93.6 4.3 %collective-permute-start = (bf16[2,3,512]{2,0,1:T(2,128)(2,1)S(1)}, bf16[2,3,512]{2,0,1:T(2,128)(2,1)S(1)}, u32[]{:S(2)}, u32[]{:S(2)}) collective-permute-start(bf16[2,3,512]{2,0,1:T(2,128)(2,1)S(1)} %slice.80), channel_id=1, source_target_pairs={{0,4},{4,8},{8,12},{12,16},{16,20},{20,24},{24,28},{28,32},{32,36}... | collective-permute-start | bytes 18440 | tf_op jit(solution)/shard_map/ppermute | solution.py:62
  102.3 14.7 %copy-start.7 = (f32[256,128]{1,0:T(8,128)S(1)}, f32[256,128]{1,0:T(8,128)}, u32[]{:S(2)}) copy-start(f32[256,128]{1,0:T(8,128)} %constant.10.clone) | copy-start | bytes 393220
  102.3 19.9 %all-to-all-start.1 = ((bf16[32,16,512]{2,1,0:T(8,128)(2,1)}), bf16[32,16,512]{2,1,0:T(8,128)(2,1)}, u32[]{:S(2)}, u32[]{:S(2)}) async-start(bf16[32,16,512]{2,1,0:T(8,128)(2,1)} %bitcast.59), calls=%async_computation.1 | async-start | bytes 1048576 | tf_op jit(solution)/shard_map/all_to_all | solution.py:54
  117.1 9.5 %copy-start.3 = (f32[256,128,1]{1,0,2:T(8,128)S(1)}, f32[256,128,1]{1,0,2:T(8,128)}, u32[]{:S(2)}) copy-start(f32[256,128,1]{1,0,2:T(8,128)} %constant.15) | copy-start | bytes 393220
  124.3 4.4 %copy-start.4 = (f32[128,128]{0,1:T(8,128)S(1)}, f32[128,128]{0,1:T(8,128)}, u32[]{:S(2)}) copy-start(f32[128,128]{0,1:T(8,128)} %constant.12.clone) | copy-start | bytes 196612
  124.3 4.4 %copy-start.5 = (f32[128,128]{0,1:T(8,128)S(1)}, f32[128,128]{0,1:T(8,128)}, u32[]{:S(2)}) copy-start(f32[128,128]{0,1:T(8,128)} %constant.11.clone) | copy-start | bytes 196612
  126.5 2.3 %copy-start = (f32[256,2048]{0,1:S(1)}, f32[256,2048]{0,1}, u32[]{:S(2)}) copy-start(f32[256,2048]{0,1} %fusion.33) | copy-start | bytes 6291460
  128.8 1.0 copy-start.1
  136.8 1.0 copy-start.6
  165.6 3.7 %copy-start.9 = (f32[512]{0:T(512)S(1)}, f32[512]{0:T(512)}, u32[]{:S(2)}) copy-start(f32[512]{0:T(512)} %param.17) | copy-start | bytes 6148
